TPU v7x, 256 devices: a whole 4x4x8 slice. The times are simulated.
256 devices in a mesh: band: 8 (over z), grid: 32 (over y, x, core).
Axes of the slice: x: 4, y: 4, z: 8, core: 2. Of those that a mesh axis runs over, the one named last changes fastest.
Arguments:
- orbitals: float32 [32, 96, 9216], P('band', 'grid'), may hold values from -6 to 6
- pair_mask: int32 [32, 4], P('band'), may hold values 0 or 1
- cycle_step: int32 [], replicated, may hold values from 1 to 7
Outputs:
- exchange_field: float32 [32, 96, 9216], P('band', 'grid')
- projection: float32 [32, 4], P('band')
All inputs are finite; a program needn't handle non-finite values. No bound on the sum of `pair_mask` on one device may be relied on, other than what follows from the above.
Results may differ from a plain program's by a relative error of at most 0.0003.
Values sent between devices are 32-bit elements; how exact they have to be, the bound alone decides.
A program may use at most 64 MiB of HBM per device.

v0:
```python
import functools
import math

import jax
import jax.numpy as jnp
import numpy as np
from jax import lax
from jax.experimental import pallas as pl
from jax.experimental.pallas import tpu as pltpu
from jax.sharding import PartitionSpec as P

N = 96
LANES = 4 * N
BOX = 16.0
SIDE = 32
EACH = 3
CHUNKS = 4
ROWS = EACH * EACH * 3
PITCH = -(-ROWS // 8) * 8
PLANE = N * N // 128
FLAT = EACH * PLANE
BANDS = 8
MESH = pl.DeviceIdType.MESH


def hartley():
    index = np.arange(N)
    angle = (index[:, None] * index[None, :] % N) * (2.0 * math.pi / N)
    return np.cos(angle) + np.sin(angle)


def two_parts(table):
    high = table.astype(jnp.bfloat16)
    low = (table - high.astype(np.float64)).astype(jnp.bfloat16)
    return high, low


def stacked(table):
    high, low = two_parts(table)
    return np.concatenate([np.concatenate([high, high], 1), np.concatenate([low, low], 1)], 0)


def tables():
    cas = hartley()
    order = np.array([EACH * (r % SIDE) + r // SIDE for r in range(N)])
    lines = np.array([4 * (r % 24) + r // 24 for r in range(N)])
    y_out = stacked(cas[order][:, lines])
    y_into = stacked(cas[lines][:, order])
    x_into = stacked(cas[:, order])
    x_out = stacked(cas[order])
    z_high, z_low = two_parts(np.kron(np.eye(4), cas))
    freq = np.arange(N)
    freq = np.where(freq * 2 >= N, freq - N, freq).astype(np.float32)
    squares = freq[:, None] ** 2 + np.tile(freq, 4)[None, :] ** 2
    pick = np.zeros((LANES, 128), np.float32)
    pick[np.arange(LANES), np.arange(LANES) // N] = 1.0
    pick = pick.astype(jnp.bfloat16)
    return y_out, y_into, x_into, x_out, z_high, z_low, squares.astype(np.float32), pick


def split(value):
    high = value.astype(jnp.bfloat16)
    low = (value - high.astype(jnp.float32)).astype(jnp.bfloat16)
    return high, low


def dot(a, b):
    return jnp.dot(a, b, preferred_element_type=jnp.float32)


def left(table, value):
    high, low = split(value)
    both = dot(table, jnp.concatenate([high, low], 0))
    return both[:N] + both[N:]


def right(value, z_high, z_low):
    high, low = split(value)
    rows = value.shape[0]
    both = dot(jnp.concatenate([high, low], 0), z_high)
    return both[:rows] + both[rows:] + dot(high, z_low)


def roll(value, shift):
    return pltpu.roll(value, shift, 1)


def lane_of(value):
    return lax.broadcasted_iota(jnp.int32, value.shape, 1)


def taken(tiles, j):
    a, b, c = tiles
    lane = lane_of(a)
    if j == 0:
        return a
    if j == 1:
        return jnp.where(lane < 32, roll(a, 32), roll(b, 32))
    if j == 2:
        return jnp.where(lane < 64, roll(b, 64), roll(c, 64))
    return roll(c, 96)


def joined(four):
    lane = lane_of(four[0])
    one, two = roll(four[1], 96), roll(four[2], 64)
    return [
        jnp.where(lane < 96, four[0], one),
        jnp.where(lane < 64, one, two),
        jnp.where(lane < 32, two, roll(four[3], 32)),
    ]


def turned(value, d):
    if d == 0:
        return value
    tiles = lane_tiles(value)
    rolled = [roll(t, 32 * d) for t in tiles]
    lane = lane_of(tiles[0])
    first = {1: 0, 2: 1, 3: 2}[d]
    return jnp.concatenate(
        [
            jnp.where(lane < 32 * d, rolled[(t + first) % 3], rolled[(t + first + 1) % 3])
            for t in range(3)
        ],
        1,
    )


def lane_tiles(value):
    return [value[:, 128 * t : 128 * t + 128] for t in range(3)]


def rows_of(ref, j, p):
    return [ref[j, pl.ds(p * PLANE + t, 24, stride=3), :] for t in range(3)]


def repeated(ref, j, p):
    tiles = rows_of(ref, j, p)
    lines = []
    for u in range(4):
        v = taken(tiles, u)
        lines.append(jnp.concatenate(joined([v, v, v, v]), 1))
    return jnp.concatenate(lines, 0)


def side_by_side(ref, p):
    tiles = [rows_of(ref, i, p) for i in range(4)]
    lines = []
    for u in range(4):
        lines.append(jnp.concatenate(joined([taken(tiles[i], u) for i in range(4)]), 1))
    return jnp.concatenate(lines, 0)


def body(
    distance,
    mask_ref, orb_ref, y_out_ref, y_into_ref, x_into_ref, x_out_ref, zh_ref, zl_ref, sq_ref, pick_ref,
    field_ref, proj_ref,
    vis, own, gram, rep, field, coulomb, send1, recv1, send2, recv2, part_send, part_recv,
    vis_sems, send_sem, recv_sem, own_sem, part_sems,
):
    me = lax.axis_index("grid")
    band = lax.axis_index("band")
    barrier = pltpu.get_barrier_semaphore()

    def greet(t, _):
        pl.semaphore_signal(barrier, inc=1, device_id={"grid": (me + t) % SIDE}, device_id_type=MESH)
        return 0

    source = (band + BANDS - distance) % BANDS
    pl.semaphore_signal(barrier, inc=1, device_id={"band": source}, device_id_type=MESH)
    lax.fori_loop(1, SIDE, greet, 0)

    def passing(j):
        return pltpu.make_async_remote_copy(
            src_ref=orb_ref.at[j],
            dst_ref=vis.at[j],
            send_sem=vis_sems.at[0, j],
            recv_sem=vis_sems.at[1, j],
            device_id={"band": (band + distance) % BANDS},
            device_id_type=MESH,
        )

    def chunk_row(p, k, b):
        return (p * EACH + k) * 3 + b

    def densities(c):
        def plane_step(p, _):
            visiting = repeated(vis, c, p)
            rep[c, p] = visiting
            value = right(own[p] * visiting, zh_ref[...], zl_ref[...])
            value = left(y_out_ref[...], value)
            for k in range(EACH):
                for b in range(3):
                    send1[c, pl.ds(chunk_row(p, k, b), SIDE, stride=PITCH), :] = value[
                        k * SIDE : (k + 1) * SIDE, b * 128 : (b + 1) * 128
                    ]
            return 0

        lax.fori_loop(0, EACH, plane_step, 0)

    def to_rows(device):
        return pl.ds(pl.multiple_of(device * PITCH, 8), ROWS)

    def exchange(way, c, send, recv):
        def one(t, _):
            to = (me + t) % SIDE
            pltpu.make_async_remote_copy(
                src_ref=send.at[c, to_rows(to)],
                dst_ref=recv.at[c, to_rows(me)],
                send_sem=send_sem.at[way, c],
                recv_sem=recv_sem.at[way, c],
                device_id={"grid": to},
                device_id_type=MESH,
            ).start()
            return 0

        lax.fori_loop(1, SIDE, one, 0)
        pltpu.make_async_copy(
            send.at[c, to_rows(me)], recv.at[c, to_rows(me)], own_sem.at[way, c]
        ).start()

    most = pl.ds(0, (SIDE - 1) * ROWS)

    def arrived(way, c, send, recv):
        pltpu.make_async_copy(
            send.at[c, to_rows(me)], recv.at[c, to_rows(me)], own_sem.at[way, c]
        ).wait()
        pltpu.make_async_copy(recv.at[c, most], recv.at[c, most], recv_sem.at[way, c]).wait()

    def sent(way, c, send):
        pltpu.make_async_copy(send.at[c, most], send.at[c, most], send_sem.at[way, c]).wait()

    def gathered(recv, c, row):
        return jnp.concatenate(
            [
                jnp.concatenate(
                    [recv[c, pl.ds(row(part, b), SIDE, stride=PITCH), :] for b in range(3)], 1
                )
                for part in range(EACH)
            ],
            0,
        )

    lane = lax.broadcasted_iota(jnp.int32, (1, LANES), 1)

    def weight_of(c):
        weights = [mask_ref[i, c].astype(jnp.float32) for i in range(4)]
        return jnp.where(
            lane < 2 * N,
            jnp.where(lane < N, weights[0], weights[1]),
            jnp.where(lane < 3 * N, weights[2], weights[3]),
        )

    def along_x(c):
        weight = weight_of(c)

        def row_step(k, _):
            value = gathered(recv1, c, lambda p, b: chunk_row(p, k, b))
            spectrum = left(x_into_ref[...], value)
            value = spectrum * coulomb[k]
            for d in range(4):
                product = value * turned(spectrum, d)
                total = product[:8]
                for r in range(8, N, 8):
                    total = total + product[r : r + 8]
                gram[d] += total * weight
            value = left(x_out_ref[...], value)
            for p in range(EACH):
                for b in range(3):
                    send2[c, pl.ds(chunk_row(p, k, b), SIDE, stride=PITCH), :] = value[
                        p * SIDE : (p + 1) * SIDE, b * 128 : (b + 1) * 128
                    ]
            return 0

        lax.fori_loop(0, EACH, row_step, 0)

    def fields(c):
        weight = weight_of(c)

        def plane_step(p, _):
            value = gathered(recv2, c, lambda k, b: chunk_row(p, k, b))
            value = left(y_into_ref[...], value)
            value = right(value, zh_ref[...], zl_ref[...])
            term = value * rep[c, p] * weight
            field[p] = field[p] - term
            return 0

        lax.fori_loop(0, EACH, plane_step, 0)

    def prepare(p, _):
        own[p] = side_by_side(orb_ref, p)
        return 0

    lax.fori_loop(0, EACH, prepare, 0)
    pl.semaphore_wait(barrier, SIDE)
    passing(0).start()
    gram[...] = jnp.zeros_like(gram)
    field[...] = jnp.zeros_like(field)
    coul = BOX * BOX / math.pi / (N * N * N)
    for k in range(EACH):
        ky = me * EACH + k
        folded = jnp.where(ky * 2 >= N, ky - N, ky).astype(jnp.float32)
        squares = sq_ref[...] + folded * folded
        coulomb[k] = jnp.where(squares > 0.5, coul / jnp.maximum(squares, 1.0), 0.0)

    def turn(c, _):
        @pl.when(c < CHUNKS)
        def _():
            passing(c).wait_recv()

            @pl.when(c + 1 < CHUNKS)
            def _():
                passing(c + 1).start()

            densities(c)
            exchange(0, c, send1, recv1)

        @pl.when(c > 0)
        def _():
            arrived(0, c - 1, send1, recv1)
            along_x(c - 1)
            exchange(1, c - 1, send2, recv2)

        return 0

    lax.fori_loop(0, CHUNKS + 1, turn, 0)
    sums = [jnp.sum(gram[d], axis=0, keepdims=True) for d in range(4)]
    sums = jnp.concatenate(sums + [jnp.zeros((4, LANES), jnp.float32)], 0)
    high = sums.astype(jnp.bfloat16)
    middle, low = split(sums - high.astype(jnp.float32))
    pick = pick_ref[...]
    sums = dot(high, pick) + dot(middle, pick) + dot(low, pick)
    part_send[...] = sums
    part_recv[me] = sums

    def tell(t, _):
        pltpu.make_async_remote_copy(
            src_ref=part_send,
            dst_ref=part_recv.at[me],
            send_sem=part_sems.at[0],
            recv_sem=part_sems.at[1],
            device_id={"grid": (me + t) % SIDE},
            device_id_type=MESH,
        ).start()
        return 0

    lax.fori_loop(1, SIDE, tell, 0)

    def finish(c, _):
        arrived(1, c, send2, recv2)
        fields(c)
        return 0

    lax.fori_loop(0, CHUNKS, finish, 0)

    def lay_out(p, _):
        tiles = [
            [field[p, 24 * u : 24 * u + 24, 128 * t : 128 * t + 128] for t in range(3)]
            for u in range(4)
        ]
        for i in range(4):
            rows = joined([taken(tiles[u], i) for u in range(4)])
            for t in range(3):
                field_ref[i, pl.ds(p * PLANE + t, 24, stride=3), :] = rows[t]
        return 0

    lax.fori_loop(0, EACH, lay_out, 0)
    for c in range(CHUNKS):
        passing(c).wait_send()
        sent(0, c, send1)
        sent(1, c, send2)
    others = part_recv.at[pl.ds(0, SIDE - 1)]
    pltpu.make_async_copy(others, others, part_sems.at[1]).wait()
    pltpu.make_async_copy(others, others, part_sems.at[0]).wait()
    sums = jnp.sum(part_recv[...], axis=0) * (-1.0 / (N * N * N))
    apart = lax.broadcasted_iota(jnp.int32, (8, 128), 0) - lax.broadcasted_iota(jnp.int32, (8, 128), 1)
    result = jnp.zeros((8, 128), jnp.float32)
    for d in range(4):
        result = jnp.where((apart + 128) % 4 == d, sums[d : d + 1], result)
    proj_ref[...] = result


def vmem(count):
    return [pl.BlockSpec(memory_space=pltpu.VMEM)] * count


def at_distance(distance, mask, orbitals, *constants):
    def scratch(*shape):
        return pltpu.VMEM(shape, jnp.float32)

    buffer = scratch(CHUNKS, SIDE * PITCH, 128)
    return pl.pallas_call(
        functools.partial(body, distance),
        out_shape=(
            jax.ShapeDtypeStruct((4, FLAT, 128), jnp.float32),
            jax.ShapeDtypeStruct((8, 128), jnp.float32),
        ),
        in_specs=[pl.BlockSpec(memory_space=pltpu.SMEM)] + vmem(1 + len(constants)),
        out_specs=tuple(vmem(2)),
        scratch_shapes=[
            scratch(4, FLAT, 128),
            scratch(EACH, N, LANES),
            scratch(4, 8, LANES),
            scratch(4, EACH, N, LANES),
            scratch(EACH, N, LANES),
            scratch(EACH, N, LANES),
            buffer, buffer, buffer, buffer,
            scratch(8, 128),
            scratch(SIDE, 8, 128),
            pltpu.SemaphoreType.DMA((2, CHUNKS)),
            pltpu.SemaphoreType.DMA((2, CHUNKS)),
            pltpu.SemaphoreType.DMA((2, CHUNKS)),
            pltpu.SemaphoreType.DMA((2, CHUNKS)),
            pltpu.SemaphoreType.DMA((2,)),
        ],
        compiler_params=pltpu.CompilerParams(
            collective_id=distance - 1, has_side_effects=True, vmem_limit_bytes=40 * 1024 * 1024
        ),
        name=f"exchange_{distance}",
    )(mask, orbitals, *constants)


def shards(orbitals, pair_mask, cycle_step):
    constants = [jnp.asarray(t) for t in tables()]
    field, projection = lax.switch(
        cycle_step - 1,
        [functools.partial(at_distance, d) for d in range(1, BANDS)],
        pair_mask,
        orbitals.reshape(4, FLAT, 128),
        *constants,
    )
    return field.reshape(4, EACH, N * N), projection[:4, :4]


def solution(mesh):
    return jax.shard_map(
        shards,
        mesh=mesh,
        in_specs=(P("band", "grid", None), P("band", None), P()),
        out_specs=(P("band", "grid", None), P("band", None)),
        check_vma=False,
    )
```

profile of v0, /device:TPU:1, one launch (start us, length us, event | category | flops | bytes accessed | tf_op | source)
XLA Modules:
  0.0 67.2 jit_solution(14283754167048818955)
XLA Ops:
  1.3 0.0 copy-start.6
  1.3 0.0 copy-start.7
  1.3 0.0 copy-start.8
  1.3 1.4 %copy.14 = f32[4,3,9216]{2,1,0:T(4,128)S(1)} copy(f32[4,3,9216]{2,0,1:T(4,128)} %param.18) | data formatting | bytes 884736 | tf_op args[0]
  2.7 0.0 copy-start
  2.7 0.0 copy-start.1
  2.7 0.0 copy-start.2
  2.7 0.0 copy-start.3
  2.7 0.0 copy-start.4
  2.7 0.0 copy-start.5
  2.8 0.2 reshape.29
  3.0 0.0 copy-done.6
  3.0 0.0 copy-done.7
  3.0 0.0 copy-done.8
  3.0 0.6 copy-done
  3.6 0.1 copy-done.1
  3.7 0.0 copy-done.2
  3.8 0.0 copy-done.3
  3.8 0.0 copy-done.4
  3.8 0.0 copy-done.5
  3.9 61.5 %conditional.1 = ((f32[4,216,128]{2,1,0:T(8,128)S(1)}, f32[8,128]{1,0:T(8,128)S(1)})) conditional(s32[]{:T(128)} %clamp.3, (s32[4,4]{1,0:T(4,128)S(1)}, f32[4,216,128]{2,1,0:T(8,128)S(1)}, bf16[192,192]{1,0:T(8,128)(2,1)S(1)}, bf16[192,192]{1,0:T(8,128)(2,1)S(1)}, bf16[192,192]{1,0:T(8,128)(2,1)S(1)}, ...), branch_computations={%region_0.0_spmd, %region_1.0_spmd, %region_2.0_spmd, %region_3.0_... | conditional | bytes 8 | solution.py:426
  3.9 61.5 %exchange_7.1 = (f32[4,216,128]{2,1,0:T(8,128)S(1)}, f32[8,128]{1,0:T(8,128)S(1)}) custom-call(s32[4,4]{1,0:T(4,128)S(1)} %get-tuple-element.228.mask_ref, f32[4,216,128]{2,1,0:T(8,128)S(1)} %get-tuple-element.229.orb_ref, bf16[192,192]{1,0:T(8,128)(2,1)S(1)} %get-tuple-element.230.y_out_ref, bf16[192,192]{1,0:T(8,128)(2,1)S(1)} %get-tuple-element.231.y_into_ref, ...), custom_call_target="tpu_custom_call" | custom-call | tf_op jit(solution)/shard_map/cond/branch_6_fun/exchange_7/pallas_call | solution.py:393
  65.3 0.6 slice.22
  65.9 0.2 reshape.30
  66.1 1.0 %copy.15 = f32[4,3,9216]{2,0,1:T(4,128)} copy(f32[4,3,9216]{2,1,0:T(4,128)S(1)} %reshape.30) | data formatting | bytes 884736
Async XLA Ops:
  1.3 1.7 %copy-start.6 = (bf16[192,192]{1,0:T(8,128)(2,1)S(1)}, bf16[192,192]{1,0:T(8,128)(2,1)}, u32[]{:S(2)}) copy-start(bf16[192,192]{1,0:T(8,128)(2,1)} %constant.24.clone) | copy-start | bytes 221188
  1.3 1.7 %copy-start.7 = (bf16[192,192]{1,0:T(8,128)(2,1)S(1)}, bf16[192,192]{1,0:T(8,128)(2,1)}, u32[]{:S(2)}) copy-start(bf16[192,192]{1,0:T(8,128)(2,1)} %constant.23.clone) | copy-start | bytes 221188
  1.3 1.7 %copy-start.8 = (s32[4,4]{1,0:T(4,128)S(1)}, s32[4,4]{1,0:T(4,128)}, u32[]{:S(2)}) copy-start(s32[4,4]{1,0:T(4,128)} %param.19) | copy-start | bytes 196
  2.7 1.0 %copy-start = (bf16[384,384]{1,0:T(8,128)(2,1)S(1)}, bf16[384,384]{1,0:T(8,128)(2,1)}, u32[]{:S(2)}) copy-start(bf16[384,384]{1,0:T(8,128)(2,1)} %constant.28.clone) | copy-start | bytes 884740
  2.7 1.0 %copy-start.1 = (bf16[384,384]{1,0:T(8,128)(2,1)S(1)}, bf16[384,384]{1,0:T(8,128)(2,1)}, u32[]{:S(2)}) copy-start(bf16[384,384]{1,0:T(8,128)(2,1)} %constant.27.clone) | copy-start | bytes 884740
  2.7 1.1 %copy-start.2 = (f32[96,384]{1,0:T(8,128)S(1)}, f32[96,384]{1,0:T(8,128)}, u32[]{:S(2)}) copy-start(f32[96,384]{1,0:T(8,128)} %constant.29.clone) | copy-start | bytes 442372
  2.7 1.1 %copy-start.3 = (bf16[384,128]{1,0:T(8,128)(2,1)S(1)}, bf16[384,128]{1,0:T(8,128)(2,1)}, u32[]{:S(2)}) copy-start(bf16[384,128]{1,0:T(8,128)(2,1)} %constant.30.clone) | copy-start | bytes 294916
  2.7 1.1 %copy-start.4 = (bf16[192,192]{1,0:T(8,128)(2,1)S(1)}, bf16[192,192]{1,0:T(8,128)(2,1)}, u32[]{:S(2)}) copy-start(bf16[192,192]{1,0:T(8,128)(2,1)} %constant.26.clone) | copy-start | bytes 221188
  2.7 1.1 %copy-start.5 = (bf16[192,192]{1,0:T(8,128)(2,1)S(1)}, bf16[192,192]{1,0:T(8,128)(2,1)}, u32[]{:S(2)}) copy-start(bf16[192,192]{1,0:T(8,128)(2,1)} %constant.25.clone) | copy-start | bytes 221188
where the time goes:
time: 67.7 us; the launch traced here: 67.2 us
  Pallas kernels  61.5 us (91%)
  local copies, waits for them, and re-layouts  4.31 us (6%)
  between operations  1.4 us (2%)
    pallas_call x1, Pallas kernels, at_distance(): pl.pallas_call(functools.partial(body, distance), out_shape=(jax.ShapeDty...  61.5 us
    unnamed x20, local copies, waits for them, and re-layouts  3.3 us

commit v1 on v0

--- a/solution.py
+++ b/solution.py
@@ -15,8 +15,13 @@
 SIDE = 32
 EACH = 3
 CHUNKS = 4
-ROWS = EACH * EACH * 3
-PITCH = -(-ROWS // 8) * 8
+UNITS = CHUNKS * EACH
+ROWS = EACH * 3
+ROOM = 16
+PITCH = EACH * ROOM
+AHEAD = 4
+X_AFTER = 6
+Y_AFTER = 12
 PLANE = N * N // 128
 FLAT = EACH * PLANE
 BANDS = 8
@@ -171,43 +176,57 @@
     pl.semaphore_signal(barrier, inc=1, device_id={"band": source}, device_id_type=MESH)
     lax.fori_loop(1, SIDE, greet, 0)
 
-    def passing(j):
+    def passing(n):
+        plane = pl.ds(pl.multiple_of(n % EACH * PLANE, 8), PLANE)
         return pltpu.make_async_remote_copy(
-            src_ref=orb_ref.at[j],
-            dst_ref=vis.at[j],
-            send_sem=vis_sems.at[0, j],
-            recv_sem=vis_sems.at[1, j],
+            src_ref=orb_ref.at[n // EACH, plane],
+            dst_ref=vis.at[n // EACH, plane],
+            send_sem=vis_sems.at[0, n],
+            recv_sem=vis_sems.at[1, n],
             device_id={"band": (band + distance) % BANDS},
             device_id_type=MESH,
         )
 
-    def chunk_row(p, k, b):
-        return (p * EACH + k) * 3 + b
-
-    def densities(c):
-        def plane_step(p, _):
-            visiting = repeated(vis, c, p)
-            rep[c, p] = visiting
-            value = right(own[p] * visiting, zh_ref[...], zl_ref[...])
-            value = left(y_out_ref[...], value)
-            for k in range(EACH):
-                for b in range(3):
-                    send1[c, pl.ds(chunk_row(p, k, b), SIDE, stride=PITCH), :] = value[
-                        k * SIDE : (k + 1) * SIDE, b * 128 : (b + 1) * 128
-                    ]
-            return 0
-
-        lax.fori_loop(0, EACH, plane_step, 0)
-
-    def to_rows(device):
-        return pl.ds(pl.multiple_of(device * PITCH, 8), ROWS)
-
-    def exchange(way, c, send, recv):
+    def unit_row(unit, part, b):
+        return unit * ROOM + part * 3 + b
+
+    def densities(n):
+        c, p = n // EACH, n % EACH
+        visiting = repeated(vis, c, p)
+        rep[c, p] = visiting
+        value = right(own[p] * visiting, zh_ref[...], zl_ref[...])
+        value = left(y_out_ref[...], value)
+        spread(send1, c, p, value)
+
+    def spread(send, c, unit, value):
+        for part in range(EACH):
+            for b in range(3):
+                send[c, pl.ds(unit_row(unit, part, b), SIDE, stride=PITCH), :] = value[
+                    part * SIDE : (part + 1) * SIDE, b * 128 : (b + 1) * 128
+                ]
+
+    def gathered(recv, c, row):
+        return jnp.concatenate(
+            [
+                jnp.concatenate(
+                    [recv[c, pl.ds(row(unit, b), SIDE, stride=PITCH), :] for b in range(3)], 1
+                )
+                for unit in range(EACH)
+            ],
+            0,
+        )
+
+    def rows_at(device, unit):
+        return pl.ds(pl.multiple_of(device * PITCH + unit * ROOM, 8), ROWS)
+
+    def exchange(way, n, send, recv):
+        c, unit = n // EACH, n % EACH
+
         def one(t, _):
             to = (me + t) % SIDE
             pltpu.make_async_remote_copy(
-                src_ref=send.at[c, to_rows(to)],
-                dst_ref=recv.at[c, to_rows(me)],
+                src_ref=send.at[c, rows_at(to, unit)],
+                dst_ref=recv.at[c, rows_at(me, unit)],
                 send_sem=send_sem.at[way, c],
                 recv_sem=recv_sem.at[way, c],
                 device_id={"grid": to},
@@ -216,31 +235,20 @@
             return 0
 
         lax.fori_loop(1, SIDE, one, 0)
-        pltpu.make_async_copy(
-            send.at[c, to_rows(me)], recv.at[c, to_rows(me)], own_sem.at[way, c]
-        ).start()
-
-    most = pl.ds(0, (SIDE - 1) * ROWS)
-
-    def arrived(way, c, send, recv):
-        pltpu.make_async_copy(
-            send.at[c, to_rows(me)], recv.at[c, to_rows(me)], own_sem.at[way, c]
-        ).wait()
-        pltpu.make_async_copy(recv.at[c, most], recv.at[c, most], recv_sem.at[way, c]).wait()
+        mine = rows_at(me, unit)
+        pltpu.make_async_copy(send.at[c, mine], recv.at[c, mine], own_sem.at[way, c]).start()
+
+    all_own = pl.ds(0, EACH * ROWS)
+    all_others = pl.ds(0, (SIDE - 1) * EACH * ROWS)
+
+    def arrived(way, c, recv):
+        own_part, other_part = recv.at[c, all_own], recv.at[c, all_others]
+        pltpu.make_async_copy(own_part, own_part, own_sem.at[way, c]).wait()
+        pltpu.make_async_copy(other_part, other_part, recv_sem.at[way, c]).wait()
 
     def sent(way, c, send):
-        pltpu.make_async_copy(send.at[c, most], send.at[c, most], send_sem.at[way, c]).wait()
-
-    def gathered(recv, c, row):
-        return jnp.concatenate(
-            [
-                jnp.concatenate(
-                    [recv[c, pl.ds(row(part, b), SIDE, stride=PITCH), :] for b in range(3)], 1
-                )
-                for part in range(EACH)
-            ],
-            0,
-        )
+        part = send.at[c, all_others]
+        pltpu.make_async_copy(part, part, send_sem.at[way, c]).wait()
 
     lane = lax.broadcasted_iota(jnp.int32, (1, LANES), 1)
 
@@ -252,41 +260,27 @@
             jnp.where(lane < 3 * N, weights[2], weights[3]),
         )
 
-    def along_x(c):
+    def along_x(n):
+        c, k = n // EACH, n % EACH
         weight = weight_of(c)
-
-        def row_step(k, _):
-            value = gathered(recv1, c, lambda p, b: chunk_row(p, k, b))
-            spectrum = left(x_into_ref[...], value)
-            value = spectrum * coulomb[k]
-            for d in range(4):
-                product = value * turned(spectrum, d)
-                total = product[:8]
-                for r in range(8, N, 8):
-                    total = total + product[r : r + 8]
-                gram[d] += total * weight
-            value = left(x_out_ref[...], value)
-            for p in range(EACH):
-                for b in range(3):
-                    send2[c, pl.ds(chunk_row(p, k, b), SIDE, stride=PITCH), :] = value[
-                        p * SIDE : (p + 1) * SIDE, b * 128 : (b + 1) * 128
-                    ]
-            return 0
-
-        lax.fori_loop(0, EACH, row_step, 0)
-
-    def fields(c):
-        weight = weight_of(c)
-
-        def plane_step(p, _):
-            value = gathered(recv2, c, lambda k, b: chunk_row(p, k, b))
-            value = left(y_into_ref[...], value)
-            value = right(value, zh_ref[...], zl_ref[...])
-            term = value * rep[c, p] * weight
-            field[p] = field[p] - term
-            return 0
-
-        lax.fori_loop(0, EACH, plane_step, 0)
+        value = gathered(recv1, c, lambda p, b: unit_row(p, k, b))
+        spectrum = left(x_into_ref[...], value)
+        value = spectrum * coulomb[k]
+        for d in range(4):
+            product = value * turned(spectrum, d)
+            total = product[:8]
+            for r in range(8, N, 8):
+                total = total + product[r : r + 8]
+            gram[d] += total * weight
+        value = left(x_out_ref[...], value)
+        spread(send2, c, k, value)
+
+    def fields(n):
+        c, p = n // EACH, n % EACH
+        value = gathered(recv2, c, lambda k, b: unit_row(k, p, b))
+        value = left(y_into_ref[...], value)
+        value = right(value, zh_ref[...], zl_ref[...])
+        field[p] = field[p] - value * rep[c, p] * weight_of(c)
 
     def prepare(p, _):
         own[p] = side_by_side(orb_ref, p)
@@ -294,7 +288,8 @@
 
     lax.fori_loop(0, EACH, prepare, 0)
     pl.semaphore_wait(barrier, SIDE)
-    passing(0).start()
+    for n in range(AHEAD):
+        passing(n).start()
     gram[...] = jnp.zeros_like(gram)
     field[...] = jnp.zeros_like(field)
     coul = BOX * BOX / math.pi / (N * N * N)
@@ -304,55 +299,69 @@
         squares = sq_ref[...] + folded * folded
         coulomb[k] = jnp.where(squares > 0.5, coul / jnp.maximum(squares, 1.0), 0.0)
 
-    def turn(c, _):
-        @pl.when(c < CHUNKS)
+    def tell_sums():
+        sums = [jnp.sum(gram[d], axis=0, keepdims=True) for d in range(4)]
+        sums = jnp.concatenate(sums + [jnp.zeros((4, LANES), jnp.float32)], 0)
+        high = sums.astype(jnp.bfloat16)
+        middle, low = split(sums - high.astype(jnp.float32))
+        pick = pick_ref[...]
+        sums = dot(high, pick) + dot(middle, pick) + dot(low, pick)
+        part_send[...] = sums
+        part_recv[me] = sums
+
+        def tell(t, _):
+            pltpu.make_async_remote_copy(
+                src_ref=part_send,
+                dst_ref=part_recv.at[me],
+                send_sem=part_sems.at[0],
+                recv_sem=part_sems.at[1],
+                device_id={"grid": (me + t) % SIDE},
+                device_id_type=MESH,
+            ).start()
+            return 0
+
+        lax.fori_loop(1, SIDE, tell, 0)
+
+    def turn(n, _):
+        @pl.when(n < UNITS)
         def _():
-            passing(c).wait_recv()
-
-            @pl.when(c + 1 < CHUNKS)
+            passing(n).wait_recv()
+
+            @pl.when(n + AHEAD < UNITS)
             def _():
-                passing(c + 1).start()
-
-            densities(c)
-            exchange(0, c, send1, recv1)
-
-        @pl.when(c > 0)
+                passing(n + AHEAD).start()
+
+            densities(n)
+            exchange(0, n, send1, recv1)
+
+        m = n - X_AFTER
+
+        @pl.when((m >= 0) & (m < UNITS))
         def _():
-            arrived(0, c - 1, send1, recv1)
-            along_x(c - 1)
-            exchange(1, c - 1, send2, recv2)
+            @pl.when(m % EACH == 0)
+            def _():
+                arrived(0, m // EACH, recv1)
+
+            along_x(m)
+            exchange(1, m, send2, recv2)
+
+        @pl.when(m == UNITS - 1)
+        def _():
+            tell_sums()
+
+        f = n - Y_AFTER
+
+        @pl.when(f >= 0)
+        def _():
+            @pl.when(f % EACH == 0)
+            def _():
+                arrived(1, f // EACH, recv2)
+
+            fields(f)
 
         return 0
 
-    lax.fori_loop(0, CHUNKS + 1, turn, 0)
-    sums = [jnp.sum(gram[d], axis=0, keepdims=True) for d in range(4)]
-    sums = jnp.concatenate(sums + [jnp.zeros((4, LANES), jnp.float32)], 0)
-    high = sums.astype(jnp.bfloat16)
-    middle, low = split(sums - high.astype(jnp.float32))
-    pick = pick_ref[...]
-    sums = dot(high, pick) + dot(middle, pick) + dot(low, pick)
-    part_send[...] = sums
-    part_recv[me] = sums
-
-    def tell(t, _):
-        pltpu.make_async_remote_copy(
-            src_ref=part_send,
-            dst_ref=part_recv.at[me],
-            send_sem=part_sems.at[0],
-            recv_sem=part_sems.at[1],
-            device_id={"grid": (me + t) % SIDE},
-            device_id_type=MESH,
-        ).start()
-        return 0
-
-    lax.fori_loop(1, SIDE, tell, 0)
-
-    def finish(c, _):
-        arrived(1, c, send2, recv2)
-        fields(c)
-        return 0
-
-    lax.fori_loop(0, CHUNKS, finish, 0)
+    lax.fori_loop(0, UNITS + Y_AFTER, turn, 0)
 
     def lay_out(p, _):
         tiles = [
@@ -366,8 +375,9 @@
         return 0
 
     lax.fori_loop(0, EACH, lay_out, 0)
+    for n in range(UNITS):
+        passing(n).wait_send()
     for c in range(CHUNKS):
-        passing(c).wait_send()
         sent(0, c, send1)
         sent(1, c, send2)
     others = part_recv.at[pl.ds(0, SIDE - 1)]
@@ -408,7 +418,7 @@
             buffer, buffer, buffer, buffer,
             scratch(8, 128),
             scratch(SIDE, 8, 128),
-            pltpu.SemaphoreType.DMA((2, CHUNKS)),
+            pltpu.SemaphoreType.DMA((2, UNITS)),
             pltpu.SemaphoreType.DMA((2, CHUNKS)),
             pltpu.SemaphoreType.DMA((2, CHUNKS)),
             pltpu.SemaphoreType.DMA((2, CHUNKS)),

time: 67.7 us -> 64.8 us (0.957)
  Pallas kernels: 61.5 us -> 59 us
    pallas_call x1, Pallas kernels: 61.5 us -> 59 us  [at_distance(): pl.pallas_call(functools.partial(body, distance), out_shape=(jax.ShapeDty...]
where the time goes in v1:
time: 64.8 us; the launch traced here: 64.7 us
  Pallas kernels  59 us (91%)
  local copies, waits for them, and re-layouts  4.31 us (7%)
  between operations  1.4 us (2%)
    pallas_call x1, Pallas kernels, at_distance(): pl.pallas_call(functools.partial(body, distance), out_shape=(jax.ShapeDty...  59 us
    unnamed x20, local copies, waits for them, and re-layouts  3.3 us

profile of v1, /device:TPU:1, one launch (start us, length us, event | category | flops | bytes accessed | tf_op | source)
XLA Modules:
  0.0 64.7 jit_solution(3842218669077474468)
XLA Ops:
  1.3 0.0 copy-start.6
  1.3 0.0 copy-start.7
  1.3 0.0 copy-start.8
  1.3 1.4 %copy.14 = f32[4,3,9216]{2,1,0:T(4,128)S(1)} copy(f32[4,3,9216]{2,0,1:T(4,128)} %param.18) | data formatting | bytes 884736 | tf_op args[0]
  2.7 0.0 copy-start
  2.7 0.0 copy-start.1
  2.7 0.0 copy-start.2
  2.7 0.0 copy-start.3
  2.7 0.0 copy-start.4
  2.7 0.0 copy-start.5
  2.8 0.2 reshape.29
  3.0 0.0 copy-done.6
  3.0 0.0 copy-done.7
  3.0 0.0 copy-done.8
  3.0 0.6 copy-done
  3.6 0.1 copy-done.1
  3.7 0.0 copy-done.2
  3.8 0.0 copy-done.3
  3.8 0.0 copy-done.4
  3.8 0.0 copy-done.5
  3.9 59.0 %conditional.1 = ((f32[4,216,128]{2,1,0:T(8,128)S(1)}, f32[8,128]{1,0:T(8,128)S(1)})) conditional(s32[]{:T(128)} %clamp.3, (s32[4,4]{1,0:T(4,128)S(1)}, f32[4,216,128]{2,1,0:T(8,128)S(1)}, bf16[192,192]{1,0:T(8,128)(2,1)S(1)}, bf16[192,192]{1,0:T(8,128)(2,1)S(1)}, bf16[192,192]{1,0:T(8,128)(2,1)S(1)}, ...), branch_computations={%region_0.0_spmd, %region_1.0_spmd, %region_2.0_spmd, %region_3.0_... | conditional | bytes 8 | solution.py:436
  3.9 59.0 %exchange_1.1 = (f32[4,216,128]{2,1,0:T(8,128)S(1)}, f32[8,128]{1,0:T(8,128)S(1)}) custom-call(s32[4,4]{1,0:T(4,128)S(1)} %get-tuple-element.156.mask_ref, f32[4,216,128]{2,1,0:T(8,128)S(1)} %get-tuple-element.157.orb_ref, bf16[192,192]{1,0:T(8,128)(2,1)S(1)} %get-tuple-element.158.y_out_ref, bf16[192,192]{1,0:T(8,128)(2,1)S(1)} %get-tuple-element.159.y_into_ref, ...), custom_call_target="tpu_custom_call" | custom-call | tf_op jit(solution)/shard_map/cond/branch_0_fun/exchange_1/pallas_call | solution.py:403
  62.8 0.6 slice.22
  63.4 0.2 reshape.30
  63.6 1.0 %copy.15 = f32[4,3,9216]{2,0,1:T(4,128)} copy(f32[4,3,9216]{2,1,0:T(4,128)S(1)} %reshape.30) | data formatting | bytes 884736
Async XLA Ops:
  1.3 1.7 %copy-start.6 = (bf16[192,192]{1,0:T(8,128)(2,1)S(1)}, bf16[192,192]{1,0:T(8,128)(2,1)}, u32[]{:S(2)}) copy-start(bf16[192,192]{1,0:T(8,128)(2,1)} %constant.24.clone) | copy-start | bytes 221188
  1.3 1.7 %copy-start.7 = (bf16[192,192]{1,0:T(8,128)(2,1)S(1)}, bf16[192,192]{1,0:T(8,128)(2,1)}, u32[]{:S(2)}) copy-start(bf16[192,192]{1,0:T(8,128)(2,1)} %constant.23.clone) | copy-start | bytes 221188
  1.3 1.7 %copy-start.8 = (s32[4,4]{1,0:T(4,128)S(1)}, s32[4,4]{1,0:T(4,128)}, u32[]{:S(2)}) copy-start(s32[4,4]{1,0:T(4,128)} %param.19) | copy-start | bytes 196
  2.7 1.0 %copy-start = (bf16[384,384]{1,0:T(8,128)(2,1)S(1)}, bf16[384,384]{1,0:T(8,128)(2,1)}, u32[]{:S(2)}) copy-start(bf16[384,384]{1,0:T(8,128)(2,1)} %constant.28.clone) | copy-start | bytes 884740
  2.7 1.0 %copy-start.1 = (bf16[384,384]{1,0:T(8,128)(2,1)S(1)}, bf16[384,384]{1,0:T(8,128)(2,1)}, u32[]{:S(2)}) copy-start(bf16[384,384]{1,0:T(8,128)(2,1)} %constant.27.clone) | copy-start | bytes 884740
  2.7 1.1 %copy-start.2 = (f32[96,384]{1,0:T(8,128)S(1)}, f32[96,384]{1,0:T(8,128)}, u32[]{:S(2)}) copy-start(f32[96,384]{1,0:T(8,128)} %constant.29.clone) | copy-start | bytes 442372
  2.7 1.1 %copy-start.3 = (bf16[384,128]{1,0:T(8,128)(2,1)S(1)}, bf16[384,128]{1,0:T(8,128)(2,1)}, u32[]{:S(2)}) copy-start(bf16[384,128]{1,0:T(8,128)(2,1)} %constant.30.clone) | copy-start | bytes 294916
  2.7 1.1 %copy-start.4 = (bf16[192,192]{1,0:T(8,128)(2,1)S(1)}, bf16[192,192]{1,0:T(8,128)(2,1)}, u32[]{:S(2)}) copy-start(bf16[192,192]{1,0:T(8,128)(2,1)} %constant.26.clone) | copy-start | bytes 221188
  2.7 1.1 %copy-start.5 = (bf16[192,192]{1,0:T(8,128)(2,1)S(1)}, bf16[192,192]{1,0:T(8,128)(2,1)}, u32[]{:S(2)}) copy-start(bf16[192,192]{1,0:T(8,128)(2,1)} %constant.25.clone) | copy-start | bytes 221188
